TPU v7x, 128 devices: a whole 4x4x4 slice. The times are simulated.
128 devices in a mesh: user: 8 (over y, core), item: 16 (over x, z).
Axes of the slice: x: 4, y: 4, z: 4, core: 2. Of those that a mesh axis runs over, the one named last changes fastest.
Arguments:
- item_factor: float32 [32768, 256], P(('item', 'user')), may hold values from -36 to 36
- context_factor: float32 [4096, 256], replicated, may hold values from -6 to 6
- tile_count: int32 [8, 16], P('user', 'item'), may hold values from 16 to 128, as said below
- tile_rows: int32 [8, 16, 128], P('user', 'item'), may hold values from 0 to 63
- tile_cols: int32 [8, 16, 128], P('user', 'item'), may hold values from 0 to 31
- tile_ctx: int32 [8, 16, 128], P('user', 'item'), may hold values from 0 to 63
- nz_offsets: int32 [8, 16, 3, 128, 512], P('user', 'item'), may hold values from 0 to 63
- nz_values: float32 [8, 16, 128, 512], P('user', 'item'), may hold values from -6 to 6
Outputs:
- user_factor: float32 [32768, 256], P(('user', 'item'))
- new_items: float32 [32768, 256], P(('item', 'user'))
Inputs may be any that keep to these rules, and one draw needn't show every extreme that they name: `tile_count`: some device has all 128 tiles live; the others 128, half, a quarter or an eighth of them.
All inputs are finite; a program needn't handle non-finite values.
Results may differ from a plain program's by a relative error of at most 0.0066.
Values may be sent and summed in bfloat16 or wider, within the bound.
A program may use at most 128 MiB of HBM per device.

v0:
```python
import jax
import jax.numpy as jnp
from jax import lax
from jax.sharding import PartitionSpec as P

TILE = 64
USR_DEV = 256
ITM_DEV = 256


def solve_rows(right_side, gram):
    lower_factor = jnp.linalg.cholesky(gram)
    partway = lax.linalg.triangular_solve(
        lower_factor, right_side, left_side=False, lower=True, transpose_a=True
    )
    return lax.linalg.triangular_solve(
        lower_factor, partway, left_side=False, lower=True, transpose_a=False
    )


def mttkrp(
    live_count,
    target_ids,
    target_offsets,
    target_tiles,
    source_tiles,
    source_ids,
    source_offsets,
    context_tiles,
    context_ids,
    context_offsets,
    values,
):
    rank_width = source_tiles.shape[2]
    per_step = 8
    steps_count = (live_count + per_step - 1) // per_step
    positions = jnp.arange(TILE, dtype=jnp.int32)

    def one_hot(offsets):
        return (offsets[..., None] == positions).astype(jnp.bfloat16)

    def advance(step_index, totals):
        first = step_index * per_step
        alive = (first + jnp.arange(per_step, dtype=jnp.int32) < live_count).astype(jnp.float32)
        step_targets = lax.dynamic_slice_in_dim(target_ids, first, per_step, 0)
        step_sources = lax.dynamic_slice_in_dim(source_ids, first, per_step, 0)
        step_contexts = lax.dynamic_slice_in_dim(context_ids, first, per_step, 0)
        step_values = lax.dynamic_slice_in_dim(values, first, per_step, 0) * alive[:, None]
        source_rows = jnp.einsum(
            "bnt,btr->bnr",
            one_hot(lax.dynamic_slice_in_dim(source_offsets, first, per_step, 0)),
            source_tiles[step_sources],
            preferred_element_type=jnp.float32,
        )
        context_rows = jnp.einsum(
            "bnt,btr->bnr",
            one_hot(lax.dynamic_slice_in_dim(context_offsets, first, per_step, 0)),
            context_tiles[step_contexts],
            preferred_element_type=jnp.float32,
        )
        terms = (step_values[:, :, None] * source_rows * context_rows).astype(jnp.bfloat16)
        placed = jnp.einsum(
            "bnt,bnr->btr",
            one_hot(lax.dynamic_slice_in_dim(target_offsets, first, per_step, 0)),
            terms,
            preferred_element_type=jnp.float32,
        )
        return totals.at[step_targets].add(placed)

    totals = jnp.zeros((target_tiles, TILE, rank_width), jnp.float32)
    totals = lax.fori_loop(0, steps_count, advance, totals)
    return totals.reshape(target_tiles * TILE, rank_width)


def local(
    item_factor, context_factor, tile_count, tile_rows, tile_cols, tile_ctx, nz_offsets, nz_values
):
    highest = lax.Precision.HIGHEST
    rank_width = item_factor.shape[1]
    user_count = lax.axis_size("user")
    item_count = lax.axis_size("item")
    user_block = USR_DEV * item_count
    item_block = ITM_DEV * user_count
    users_total = user_block * user_count
    items_total = item_block * item_count
    live_count = tile_count[0, 0]
    row_ids = tile_rows[0, 0]
    col_ids = tile_cols[0, 0]
    ctx_ids = tile_ctx[0, 0]
    offsets = nz_offsets[0, 0]
    values = nz_values[0, 0]
    context_tiles = context_factor.astype(jnp.bfloat16).reshape(-1, TILE, rank_width)
    context_gram = jnp.dot(
        context_factor.T, context_factor, precision=highest, preferred_element_type=jnp.float32
    )
    item_gram = lax.psum(
        jnp.dot(item_factor.T, item_factor, precision=highest, preferred_element_type=jnp.float32),
        ("user", "item"),
    )
    item_local = lax.all_gather(item_factor.astype(jnp.bfloat16), "user", axis=0, tiled=True)
    partial_users = mttkrp(
        live_count,
        row_ids,
        offsets[0],
        user_block // TILE,
        item_local.reshape(-1, TILE, rank_width),
        col_ids,
        offsets[1],
        context_tiles,
        ctx_ids,
        offsets[2],
        values,
    )
    user_system = item_gram * context_gram
    owned_sum = lax.psum_scatter(partial_users, "item", scatter_dimension=0, tiled=True)
    raw_rows = solve_rows(owned_sum, user_system)
    raw_gram = lax.psum(
        jnp.dot(raw_rows.T, raw_rows, precision=highest, preferred_element_type=jnp.float32),
        ("user", "item"),
    )
    column_scale = jnp.sqrt(users_total / (jnp.diagonal(raw_gram) + 1e-06))
    owned_users = raw_rows * column_scale
    user_local = lax.all_gather(owned_users.astype(jnp.bfloat16), "item", axis=0, tiled=True)
    user_gram = raw_gram * column_scale[:, None] * column_scale[None, :]
    partial_items = mttkrp(
        live_count,
        col_ids,
        offsets[1],
        item_block // TILE,
        user_local.reshape(-1, TILE, rank_width),
        row_ids,
        offsets[0],
        context_tiles,
        ctx_ids,
        offsets[2],
        values,
    )
    owned_items = lax.psum_scatter(partial_items, "user", scatter_dimension=0, tiled=True)
    item_raw = solve_rows(owned_items, user_gram * context_gram)
    item_squares = lax.psum(jnp.sum(item_raw * item_raw, axis=0), ("user", "item"))
    new_items = item_raw * jnp.sqrt(items_total / (item_squares + 1e-06))
    return (owned_users, new_items)


def solution(mesh):
    in_specs = (
        P(("item", "user"), None),
        P(),
        P("user", "item"),
        P("user", "item", None),
        P("user", "item", None),
        P("user", "item", None),
        P("user", "item", None, None, None),
        P("user", "item", None, None),
    )
    out_specs = (P(("user", "item"), None), P(("item", "user"), None))
    return jax.shard_map(local, mesh=mesh, in_specs=in_specs, out_specs=out_specs, check_vma=False)
```

profile of v0, /device:TPU:1, one launch (start us, length us, event | category | flops | bytes accessed | tf_op | source)
XLA Modules:
  0.0 921.8 jit_solution(2475890599702103652)
XLA Ops:
  14.8 2.4 convert_element_type.36
  17.2 20.4 %all-gather.3.cloned.1.call-done = bf16[2048,256]{1,0:T(8,128)(2,1)} async-done(((bf16[256,256]{1,0:T(8,128)(2,1)}), bf16[2048,256]{1,0:T(8,128)(2,1)}) %all-gather.3.cloned.1.call-update) | async-done | bytes 1048592 | tf_op jit(solution)/shard_map/all_gather | solution.py:100
  37.6 2.4 broadcast_in_dim.32
  40.1 115.4 %while.32 = (s32[]{:T(128)}, f32[64,64,256]{2,1,0:T(8,128)}, s32[]{:T(128)}, s32[128]{0:T(128)S(1)}, s32[128,512]{1,0:T(8,128)}, /*index=5*/f32[128,512]{1,0:T(8...) while((s32[]{:T(128)}, f32[64,64,256]{2,1,0:T(8,128)}, ...), condition=%wide.region_7.9_spmd.clone.clone, body=%wide.region_5.8_spmd.clone.clone.sunk | while | flops 406722656 | bytes 12264079 | solution.py:71
  42.8 2.7 fusion.82
  48.3 3.6 fusion.83
  51.9 2.7 scatter_fusion
  57.2 2.7 fusion.82
  62.7 3.6 fusion.83
  66.3 2.7 scatter_fusion
  71.6 2.7 fusion.82
  77.1 3.6 fusion.83
  80.7 2.7 scatter_fusion
  86.0 2.7 fusion.82
  91.5 3.6 fusion.83
  95.1 2.7 scatter_fusion
  100.4 2.7 fusion.82
  105.9 3.6 fusion.83
  109.5 2.7 scatter_fusion
  114.9 2.7 fusion.82
  120.3 3.6 fusion.83
  123.9 2.7 scatter_fusion
  129.3 2.7 fusion.82
  134.8 3.6 fusion.83
  138.4 2.7 scatter_fusion
  143.8 2.7 fusion.82
  149.2 3.6 fusion.83
  152.8 2.6 scatter_fusion
  156.2 3.7 all-reduce.4.cloned.1.call-done
  159.9 10.2 %fusion.46 = (f32[256,256]{0,1:T(8,128)S(1)}, f32[256,256]{0,1:T(8,128)S(1)}) fusion(f32[256,256]{0,1:T(8,128)} %all-reduce.4.cloned.1.call-done, f32[4096,256]{1,0:T(8,128)} %param.18), kind=kOutput, calls=%fused_computation.122 | convolution fusion | flops 3221291008 | bytes 4980736 | tf_op jit(solution)/shard_map/dot_general | solution.py:93
  170.3 11.7 %cholesky.130 = f32[128,128]{1,0:T(8,128)S(1)} custom-call(f32[128,128]{1,0:T(8,128)S(1)} %cholesky.194), custom_call_target="Cholesky" | custom-call | tf_op jit(solution)/shard_map/jit(cholesky)/cholesky | solution.py:12
  182.0 9.9 %custom-call.19 = f32[1,128,128]{1,2,0:T(8,128)S(1)} custom-call(f32[1,128,128]{2,1,0:T(8,128)S(1)} %get-tuple-element.432), custom_call_target="InvertDiagBlocksLowerTriangular" | custom-call | tf_op jit(solution)/shard_map/jit(cholesky)/cholesky | solution.py:12
  192.5 11.7 %cholesky.147 = f32[128,128]{1,0:T(8,128)S(1)} custom-call(f32[128,128]{1,0:T(8,128)S(1)} %convolution_subtract_fusion.5), custom_call_target="Cholesky" | custom-call | tf_op jit(solution)/shard_map/jit(cholesky)/cholesky | solution.py:12
  206.2 3.9 while.34
  210.2 19.7 %custom-call.20 = f32[2,128,128]{1,2,0:T(8,128)S(1)} custom-call(f32[2,128,128]{2,1,0:T(8,128)S(1)} %get-tuple-element.319), custom_call_target="InvertDiagBlocksLowerTriangular" | custom-call | tf_op jit(solution)/shard_map/triangular_solve/custom-call.0 | solution.py:13
  229.8 116.2 %reduce-scatter.3.cloned.1.call-done = f32[256,256]{1,0:T(8,128)} async-done(((f32[4096,256]{1,0:T(8,128)}), f32[256,256]{1,0:T(8,128)}) %reduce-scatter.3.cloned.1.call-update) | async-done | bytes 262160 | tf_op jit(solution)/shard_map/reduce_scatter | solution.py:115
  351.0 142.3 %all-reduce.6.cloned.1.call-done = f32[256,256]{0,1:T(8,128)} async-done(((f32[256,256]{0,1:T(8,128)}), f32[256,256]{0,1:T(8,128)}) %all-reduce.6.cloned.1.call-update) | async-done | bytes 262160 | tf_op jit(solution)/shard_map/psum | solution.py:117
  493.3 2.6 gather_fusion.4
  497.8 44.1 %all-gather.5.cloned.1.call-done = bf16[4096,256]{0,1:T(8,128)(2,1)} async-done(((bf16[256,256]{0,1:T(8,128)(2,1)}), bf16[4096,256]{0,1:T(8,128)(2,1)}) %all-gather.5.cloned.1.call-update) | async-done | bytes 2097168 | tf_op jit(solution)/shard_map/all_gather | solution.py:123
  541.9 4.1 copy.25
  546.3 118.1 %while.33 = (s32[]{:T(128)}, f32[32,64,256]{2,1,0:T(8,128)S(1)}, s32[]{:T(128)}, s32[128]{0:T(128)S(1)}, s32[128,512]{1,0:T(8,128)}, /*index=5*/f32[128,512]{1,0...) while((s32[]{:T(128)}, f32[32,64,256]{2,1,0:T(8,128)S(1)}, ...), condition=%wide.region_12.16_spmd.clone.clone, body=%wide.region_10.0_spmd.clone.clone.sunk | while | flops 406722656 | bytes 12264079 | solution.py:71
  549.6 2.7 fusion.86
  556.6 3.6 fusion.87
  564.3 2.7 fusion.86
  571.3 3.6 fusion.87
  579.0 2.7 fusion.86
  586.1 3.6 fusion.87
  593.8 2.7 fusion.86
  600.8 3.6 fusion.87
  608.5 2.7 fusion.86
  615.5 3.6 fusion.87
  623.2 2.7 fusion.86
  630.3 3.6 fusion.87
  638.0 2.7 fusion.86
  645.0 3.6 fusion.87
  652.7 2.7 fusion.86
  659.7 3.6 fusion.87
  666.8 11.7 %cholesky.164 = f32[128,128]{1,0:T(8,128)S(1)} custom-call(f32[128,128]{1,0:T(8,128)S(1)} %cholesky.197), custom_call_target="Cholesky" | custom-call | tf_op jit(solution)/shard_map/jit(cholesky)/cholesky | solution.py:12
  678.5 9.8 %custom-call.22 = f32[1,128,128]{1,2,0:T(8,128)S(1)} custom-call(f32[1,128,128]{2,1,0:T(8,128)S(1)} %get-tuple-element.428), custom_call_target="InvertDiagBlocksLowerTriangular" | custom-call | tf_op jit(solution)/shard_map/jit(cholesky)/cholesky | solution.py:12
  688.8 11.7 %cholesky.181 = f32[128,128]{1,0:T(8,128)S(1)} custom-call(f32[128,128]{1,0:T(8,128)S(1)} %convolution_subtract_fusion.4), custom_call_target="Cholesky" | custom-call | tf_op jit(solution)/shard_map/jit(cholesky)/cholesky | solution.py:12
  703.1 4.1 while.35
  707.2 19.7 %custom-call.23 = f32[2,128,128]{1,2,0:T(8,128)S(1)} custom-call(f32[2,128,128]{2,1,0:T(8,128)S(1)} %get-tuple-element.321), custom_call_target="InvertDiagBlocksLowerTriangular" | custom-call | tf_op jit(solution)/shard_map/triangular_solve/custom-call.0 | solution.py:13
  726.9 87.1 %reduce-scatter.5.cloned.1.call-done = f32[256,256]{1,0:T(8,128)} async-done(((f32[2048,256]{1,0:T(8,128)}), f32[256,256]{1,0:T(8,128)}) %reduce-scatter.5.cloned.1.call-update) | async-done | bytes 262160 | tf_op jit(solution)/shard_map/reduce_scatter | solution.py:138
  817.9 95.6 %psum.23 = f32[256]{0:T(256)S(1)} all-reduce(f32[256]{0:T(256)S(1)} %multiply_reduce_fusion), channel_id=1, replica_groups=mesh['user'=8,'item'=16] {'user','item'}, use_global_device_ids=true, to_apply=%region_15.19 | all-reduce | flops 256 | bytes 2048 | tf_op jit(solution)/shard_map/psum | solution.py:140
  (256 shorter events, 142.5 us)
Async XLA Ops:
  8.0 29.6 %all-gather.3.cloned.1.call-start = ((), (), s32[]{:S(2)}) async-start(), calls=%async_computation.3 | async-start | bytes 1179648 | tf_op jit(solution)/shard_map/all_gather | solution.py:100
  9.7 150.2 %all-reduce.4.cloned.1.call-start = ((), (), s32[]{:S(2)}) async-start(), calls=%async_computation.2 | async-start | bytes 524288 | tf_op jit(solution)/shard_map/psum | solution.py:96
  12.1 334.0 %reduce-scatter.3.cloned.1.call-start = ((), (), s32[]{:S(2)}) async-start(), calls=%async_computation.4 | async-start | bytes 4456448 | tf_op jit(solution)/shard_map/reduce_scatter | solution.py:115
  14.8 25.3 %copy-start.4 = (s32[1,1,128]{2,1,0:T(1,128)S(1)}, s32[1,1,128]{2,1,0:T(1,128)}, u32[]{:S(2)}) copy-start(s32[1,1,128]{2,1,0:T(1,128)} %param.22) | copy-start | bytes 1540
  14.8 25.3 %copy-start.5 = (s32[1,1,128]{2,1,0:T(1,128)S(1)}, s32[1,1,128]{2,1,0:T(1,128)}, u32[]{:S(2)}) copy-start(s32[1,1,128]{2,1,0:T(1,128)} %param.20) | copy-start | bytes 1540
  14.8 25.3 %copy-start.6 = (s32[1,1,128]{2,1,0:T(1,128)S(1)}, s32[1,1,128]{2,1,0:T(1,128)}, u32[]{:S(2)}) copy-start(s32[1,1,128]{2,1,0:T(1,128)} %param.21) | copy-start | bytes 1540
  155.5 0.7 copy-start.3
  155.5 14.6 %copy-start.1 = (bf16[64,64,256]{2,1,0:T(8,128)(2,1)}, bf16[64,64,256]{2,1,0:T(8,128)(2,1)S(1)}, u32[]{:S(2)}) copy-start(bf16[64,64,256]{2,1,0:T(8,128)(2,1)S(1)} %get-tuple-element.818) | copy-start | bytes 6291460
  155.5 337.8 %all-reduce.6.cloned.1.call-start = ((), (), s32[]{:S(2)}) async-start(), calls=%async_computation.5 | async-start | bytes 524288 | tf_op jit(solution)/shard_map/psum | solution.py:117
  350.9 191.0 %all-gather.5.cloned.1.call-start = ((), (), s32[]{:S(2)}) async-start(), calls=%async_computation.6 | async-start | bytes 2228224 | tf_op jit(solution)/shard_map/all_gather | solution.py:123
  497.8 316.2 %reduce-scatter.5.cloned.1.call-start = ((), (), s32[]{:S(2)}) async-start(), calls=%async_computation.7 | async-start | bytes 2359296 | tf_op jit(solution)/shard_map/reduce_scatter | solution.py:138
  546.3 119.5 %copy-start.2 = (f32[256,256]{0,1:T(8,128)S(1)}, f32[256,256]{0,1:T(8,128)}, u32[]{:S(2)}) copy-start(f32[256,256]{0,1:T(8,128)} %get-tuple-element.409) | copy-start | bytes 786436
  664.3 1.4 copy-start
Sparse Core Ops, SparseCore 0:
  10.5 27.0 all-gather.2
  155.6 190.4 reduce-scatter.2
  497.9 43.9 all-gather.4
  665.8 148.1 reduce-scatter.4
Sparse Core Ops, SparseCore 1:
  14.9 144.9 all-reduce.3
  351.0 142.2 all-reduce.5
where the time goes:
time: 936 us; the launch traced here: 922 us
  waiting for transfers between devices  414 us (44%)
  other arithmetic  170 us (18%)
  matrix products  122 us (13%)
  local copies, waits for them, and re-layouts  99 us (11%)
  blocking collectives  95.6 us (10%)
  between operations  18.9 us (2%)
    psum x1, waiting for transfers between devices, local(): lax.psum(jnp.dot(raw_rows.T, raw_rows, precision=highest, preferred_eleme...  142 us
    reduce_scatter x1, waiting for transfers between devices, local(): lax.psum_scatter(partial_users, 'item', scatter_dimension=0, tiled=True)  116 us
    psum x1, blocking collectives, local(): lax.psum(jnp.sum(item_raw * item_raw, axis=0), ('user', 'item'))  95.6 us
    reduce_scatter x1, waiting for transfers between devices, local(): lax.psum_scatter(partial_items, 'user', scatter_dimension=0, tiled=True)  87.1 us
    another operation x13, other arithmetic, solve_rows(): lower_factor = jnp.linalg.cholesky(gram)  68.7 us
    dot_general x16, matrix products, advance(): jnp.einsum('bnt,bnr->btr', one_hot(lax.dynamic_slice_in_dim(target_offset...  57.1 us
    all_gather x1, waiting for transfers between devices, local(): lax.all_gather(owned_users.astype(jnp.bfloat16), 'item', axis=0, tiled=True)  44.1 us
    dot_general x16, matrix products, advance(): jnp.einsum('bnt,btr->bnr', one_hot(lax.dynamic_slice_in_dim(source_offset...  43.4 us
  transfers between devices with their start and end apart: 6, of which 6 were waited for; matrix products, arithmetic and copies ran while one was open for 27% of the time, Pallas kernels for 0%

commit v1 on v0

--- a/solution.py
+++ b/solution.py
@@ -137,7 +137,7 @@
     )
     owned_items = lax.psum_scatter(partial_items, "user", scatter_dimension=0, tiled=True)
     item_raw = solve_rows(owned_items, user_gram * context_gram)
-    item_squares = lax.psum(jnp.sum(item_raw * item_raw, axis=0), ("user", "item"))
+    item_squares = lax.psum(lax.psum(jnp.sum(item_raw * item_raw, axis=0), "user"), "item")
     new_items = item_raw * jnp.sqrt(items_total / (item_squares + 1e-06))
     return (owned_users, new_items)
 

time: 936 us -> 920 us (0.983)
  the two profiles are of different devices: /device:TPU:1 before, /device:TPU:0 now
where the time goes in v1:
time: 920 us; the launch traced here: 906 us
  waiting for transfers between devices  533 us (58%)
  other arithmetic  142 us (15%)
  blocking collectives  77.6 us (8%)
  matrix products  72.2 us (8%)
  local copies, waits for them, and re-layouts  60.7 us (7%)
  between operations  18.9 us (2%)
    reduce_scatter x1, waiting for transfers between devices, local(): lax.psum_scatter(partial_items, 'user', scatter_dimension=0, tiled=True)  148 us
    psum x1, waiting for transfers between devices, local(): lax.psum(jnp.dot(raw_rows.T, raw_rows, precision=highest, preferred_eleme...  141 us
    reduce_scatter x1, waiting for transfers between devices, local(): lax.psum_scatter(partial_users, 'item', scatter_dimension=0, tiled=True)  118 us
    another operation x13, other arithmetic, solve_rows(): lower_factor = jnp.linalg.cholesky(gram)  68.7 us
    psum x1, blocking collectives, local(): lax.psum(lax.psum(jnp.sum(item_raw * item_raw, axis=0), 'user'), 'item')  64.9 us
    psum x1, waiting for transfers between devices, local(): lax.psum(jnp.dot(item_factor.T, item_factor, precision=highest, preferred...  61.9 us
    all_gather x1, waiting for transfers between devices, local(): lax.all_gather(owned_users.astype(jnp.bfloat16), 'item', axis=0, tiled=True)  44.9 us
    another operation x5, other arithmetic, solve_rows(): lax.linalg.triangular_solve(lower_factor, right_side, left_side=False, lo...  39.4 us
  transfers between devices with their start and end apart: 6, of which 6 were waited for; matrix products, arithmetic and copies ran while one was open for 22% of the time, Pallas kernels for 0%

profile of v1, /device:TPU:0, one launch (start us, length us, event | category | flops | bytes accessed | tf_op | source)
XLA Modules:
  0.0 906.1 jit_solution(11333845710198201042)
XLA Ops:
  8.0 1.6 convert_element_type.35
  9.7 2.3 fusion.47
  12.8 2.0 slice_bitcast_fusion
  14.8 2.4 convert_element_type.36
  17.2 19.2 %all-gather.3.cloned.1.call-done = bf16[2048,256]{1,0:T(8,128)(2,1)} async-done(((bf16[256,256]{1,0:T(8,128)(2,1)}), bf16[2048,256]{1,0:T(8,128)(2,1)}) %all-gather.3.cloned.1.call-update) | async-done | bytes 1048592 | tf_op jit(solution)/shard_map/all_gather | solution.py:100
  36.5 2.4 broadcast_in_dim.32
  38.9 57.7 %while.32 = (s32[]{:T(128)}, f32[64,64,256]{2,1,0:T(8,128)}, s32[]{:T(128)}, s32[128]{0:T(128)S(1)}, s32[128,512]{1,0:T(8,128)}, /*index=5*/f32[128,512]{1,0:T(8...) while((s32[]{:T(128)}, f32[64,64,256]{2,1,0:T(8,128)}, ...), condition=%wide.region_7.9_spmd.clone.clone, body=%wide.region_5.8_spmd.clone.clone.sunk | while | flops 406722656 | bytes 12264079 | solution.py:71
  39.1 1.8 gather_fusion
  41.6 2.7 fusion.82
  47.1 3.6 fusion.83
  50.7 2.6 scatter_fusion
  53.5 1.8 gather_fusion
  56.0 2.7 fusion.82
  61.5 3.6 fusion.83
  65.1 2.7 scatter_fusion
  67.9 1.8 gather_fusion
  70.4 2.7 fusion.82
  75.9 3.6 fusion.83
  79.5 2.6 scatter_fusion
  82.3 1.8 gather_fusion
  84.8 2.7 fusion.82
  90.3 3.6 fusion.83
  93.9 2.7 scatter_fusion
  97.3 61.9 %all-reduce.4.cloned.1.call-done = f32[256,256]{0,1:T(8,128)} async-done(((f32[256,256]{0,1:T(8,128)}), f32[256,256]{0,1:T(8,128)}) %all-reduce.4.cloned.1.call-update) | async-done | bytes 262160 | tf_op jit(solution)/shard_map/psum | solution.py:96
  159.2 10.2 %fusion.46 = (f32[256,256]{0,1:T(8,128)S(1)}, f32[256,256]{0,1:T(8,128)S(1)}) fusion(f32[256,256]{0,1:T(8,128)} %all-reduce.4.cloned.1.call-done, f32[4096,256]{1,0:T(8,128)} %param.18), kind=kOutput, calls=%fused_computation.122 | convolution fusion | flops 3221291008 | bytes 4980736 | tf_op jit(solution)/shard_map/dot_general | solution.py:93
  169.6 11.7 %cholesky.130 = f32[128,128]{1,0:T(8,128)S(1)} custom-call(f32[128,128]{1,0:T(8,128)S(1)} %cholesky.194), custom_call_target="Cholesky" | custom-call | tf_op jit(solution)/shard_map/jit(cholesky)/cholesky | solution.py:12
  181.4 9.9 %custom-call.19 = f32[1,128,128]{1,2,0:T(8,128)S(1)} custom-call(f32[1,128,128]{2,1,0:T(8,128)S(1)} %get-tuple-element.432), custom_call_target="InvertDiagBlocksLowerTriangular" | custom-call | tf_op jit(solution)/shard_map/jit(cholesky)/cholesky | solution.py:12
  191.8 11.7 %cholesky.147 = f32[128,128]{1,0:T(8,128)S(1)} custom-call(f32[128,128]{1,0:T(8,128)S(1)} %convolution_subtract_fusion.5), custom_call_target="Cholesky" | custom-call | tf_op jit(solution)/shard_map/jit(cholesky)/cholesky | solution.py:12
  205.6 3.9 while.34
  209.5 19.7 %custom-call.20 = f32[2,128,128]{1,2,0:T(8,128)S(1)} custom-call(f32[2,128,128]{2,1,0:T(8,128)S(1)} %get-tuple-element.319), custom_call_target="InvertDiagBlocksLowerTriangular" | custom-call | tf_op jit(solution)/shard_map/triangular_solve/custom-call.0 | solution.py:13
  229.2 117.8 %reduce-scatter.3.cloned.1.call-done = f32[256,256]{1,0:T(8,128)} async-done(((f32[4096,256]{1,0:T(8,128)}), f32[256,256]{1,0:T(8,128)}) %reduce-scatter.3.cloned.1.call-update) | async-done | bytes 262160 | tf_op jit(solution)/shard_map/reduce_scatter | solution.py:115
  351.9 140.8 %all-reduce.6.cloned.1.call-done = f32[256,256]{0,1:T(8,128)} async-done(((f32[256,256]{0,1:T(8,128)}), f32[256,256]{0,1:T(8,128)}) %all-reduce.6.cloned.1.call-update) | async-done | bytes 262160 | tf_op jit(solution)/shard_map/psum | solution.py:117
  492.7 2.6 gather_fusion.4
  495.3 1.8 fusion.42
  497.2 44.9 %all-gather.5.cloned.1.call-done = bf16[4096,256]{0,1:T(8,128)(2,1)} async-done(((bf16[256,256]{0,1:T(8,128)(2,1)}), bf16[4096,256]{0,1:T(8,128)(2,1)}) %all-gather.5.cloned.1.call-update) | async-done | bytes 2097168 | tf_op jit(solution)/shard_map/all_gather | solution.py:123
  542.1 4.1 copy.25
  546.4 59.1 %while.33 = (s32[]{:T(128)}, f32[32,64,256]{2,1,0:T(8,128)S(1)}, s32[]{:T(128)}, s32[128]{0:T(128)S(1)}, s32[128,512]{1,0:T(8,128)}, /*index=5*/f32[128,512]{1,0...) while((s32[]{:T(128)}, f32[32,64,256]{2,1,0:T(8,128)S(1)}, ...), condition=%wide.region_12.16_spmd.clone.clone, body=%wide.region_10.0_spmd.clone.clone.sunk | while | flops 406722656 | bytes 12264079 | solution.py:71
  546.8 2.2 gather_fusion.2
  549.7 2.7 fusion.86
  552.4 2.2 gather_fusion.3
  556.7 3.6 fusion.87
  561.5 2.2 gather_fusion.2
  564.4 2.7 fusion.86
  567.1 2.2 gather_fusion.3
  571.5 3.6 fusion.87
  576.2 2.2 gather_fusion.2
  579.2 2.7 fusion.86
  581.9 2.2 gather_fusion.3
  586.2 3.6 fusion.87
  591.0 2.2 gather_fusion.2
  593.9 2.7 fusion.86
  596.6 2.2 gather_fusion.3
  600.9 3.6 fusion.87
  605.5 1.3 copy-done
  608.0 11.7 %cholesky.164 = f32[128,128]{1,0:T(8,128)S(1)} custom-call(f32[128,128]{1,0:T(8,128)S(1)} %cholesky.197), custom_call_target="Cholesky" | custom-call | tf_op jit(solution)/shard_map/jit(cholesky)/cholesky | solution.py:12
  619.7 9.8 %custom-call.22 = f32[1,128,128]{1,2,0:T(8,128)S(1)} custom-call(f32[1,128,128]{2,1,0:T(8,128)S(1)} %get-tuple-element.428), custom_call_target="InvertDiagBlocksLowerTriangular" | custom-call | tf_op jit(solution)/shard_map/jit(cholesky)/cholesky | solution.py:12
  630.0 11.7 %cholesky.181 = f32[128,128]{1,0:T(8,128)S(1)} custom-call(f32[128,128]{1,0:T(8,128)S(1)} %convolution_subtract_fusion.4), custom_call_target="Cholesky" | custom-call | tf_op jit(solution)/shard_map/jit(cholesky)/cholesky | solution.py:12
  644.3 4.1 while.35
  645.2 1.3 bitcast_dynamic-update-slice_fusion.5
  647.1 1.3 bitcast_dynamic-update-slice_fusion.5
  648.4 19.7 %custom-call.23 = f32[2,128,128]{1,2,0:T(8,128)S(1)} custom-call(f32[2,128,128]{2,1,0:T(8,128)S(1)} %get-tuple-element.321), custom_call_target="InvertDiagBlocksLowerTriangular" | custom-call | tf_op jit(solution)/shard_map/triangular_solve/custom-call.0 | solution.py:13
  668.1 148.2 %reduce-scatter.5.cloned.1.call-done = f32[256,256]{1,0:T(8,128)} async-done(((f32[2048,256]{1,0:T(8,128)}), f32[256,256]{1,0:T(8,128)}) %reduce-scatter.5.cloned.1.call-update) | async-done | bytes 262160 | tf_op jit(solution)/shard_map/reduce_scatter | solution.py:138
  820.1 12.7 %psum.30 = f32[256]{0:T(256)S(1)} all-reduce(f32[256]{0:T(256)S(1)} %multiply_reduce_fusion), channel_id=1, replica_groups=mesh['user'=8,'item'=16] {'user'}, use_global_device_ids=true, to_apply=%region_15.19 | all-reduce | flops 256 | bytes 2048 | tf_op jit(solution)/shard_map/psum | solution.py:140
  832.8 64.9 %psum.31 = f32[256]{0:T(256)S(1)} all-reduce(f32[256]{0:T(256)S(1)} %psum.30), channel_id=1, replica_groups=mesh['user'=8,'item'=16] {'item'}, use_global_device_ids=true, to_apply=%region_16.20 | all-reduce | flops 256 | bytes 2048 | tf_op jit(solution)/shard_map/psum | solution.py:140
  (153 shorter events, 51.2 us)
Async XLA Ops:
  8.0 28.5 %all-gather.3.cloned.1.call-start = ((), (), s32[]{:S(2)}) async-start(), calls=%async_computation.3 | async-start | bytes 1179648 | tf_op jit(solution)/shard_map/all_gather | solution.py:100
  9.7 149.5 %all-reduce.4.cloned.1.call-start = ((), (), s32[]{:S(2)}) async-start(), calls=%async_computation.2 | async-start | bytes 524288 | tf_op jit(solution)/shard_map/psum | solution.py:96
  12.1 334.9 %reduce-scatter.3.cloned.1.call-start = ((), (), s32[]{:S(2)}) async-start(), calls=%async_computation.4 | async-start | bytes 4456448 | tf_op jit(solution)/shard_map/reduce_scatter | solution.py:115
  14.8 24.1 %copy-start.4 = (s32[1,1,128]{2,1,0:T(1,128)S(1)}, s32[1,1,128]{2,1,0:T(1,128)}, u32[]{:S(2)}) copy-start(s32[1,1,128]{2,1,0:T(1,128)} %param.22) | copy-start | bytes 1540
  14.8 24.1 %copy-start.5 = (s32[1,1,128]{2,1,0:T(1,128)S(1)}, s32[1,1,128]{2,1,0:T(1,128)}, u32[]{:S(2)}) copy-start(s32[1,1,128]{2,1,0:T(1,128)} %param.20) | copy-start | bytes 1540
  14.8 24.1 %copy-start.6 = (s32[1,1,128]{2,1,0:T(1,128)S(1)}, s32[1,1,128]{2,1,0:T(1,128)}, u32[]{:S(2)}) copy-start(s32[1,1,128]{2,1,0:T(1,128)} %param.21) | copy-start | bytes 1540
  96.6 0.7 copy-start.3
  96.6 72.8 %copy-start.1 = (bf16[64,64,256]{2,1,0:T(8,128)(2,1)}, bf16[64,64,256]{2,1,0:T(8,128)(2,1)S(1)}, u32[]{:S(2)}) copy-start(bf16[64,64,256]{2,1,0:T(8,128)(2,1)S(1)} %get-tuple-element.818) | copy-start | bytes 6291460
  96.6 396.0 %all-reduce.6.cloned.1.call-start = ((), (), s32[]{:S(2)}) async-start(), calls=%async_computation.5 | async-start | bytes 524288 | tf_op jit(solution)/shard_map/psum | solution.py:117
  351.8 190.2 %all-gather.5.cloned.1.call-start = ((), (), s32[]{:S(2)}) async-start(), calls=%async_computation.6 | async-start | bytes 2228224 | tf_op jit(solution)/shard_map/all_gather | solution.py:123
  497.1 319.1 %reduce-scatter.5.cloned.1.call-start = ((), (), s32[]{:S(2)}) async-start(), calls=%async_computation.7 | async-start | bytes 2359296 | tf_op jit(solution)/shard_map/reduce_scatter | solution.py:138
  546.4 60.5 %copy-start.2 = (f32[256,256]{0,1:T(8,128)S(1)}, f32[256,256]{0,1:T(8,128)}, u32[]{:S(2)}) copy-start(f32[256,256]{0,1:T(8,128)} %get-tuple-element.409) | copy-start | bytes 786436
  605.5 1.4 copy-start
Sparse Core Ops, SparseCore 0:
  10.5 25.8 all-gather.2
  96.8 250.1 reduce-scatter.2
  497.2 44.7 all-gather.4
  607.0 209.1 reduce-scatter.4
Sparse Core Ops, SparseCore 1:
  14.9 144.3 all-reduce.3
  351.9 140.7 all-reduce.5
